TPU v7x, 256 devices: a whole 4x4x8 slice. The times are simulated.
256 devices in a mesh: chan: 64 (over z, y, core), tm: 4 (over x).
Axes of the slice: x: 4, y: 4, z: 8, core: 2. Of those that a mesh axis runs over, the one named last changes fastest.
Arguments:
- traces: float32 [5120, 8192], P('chan', 'tm'), may hold values from -6 to 6
- fir_taps: float32 [65], replicated, may hold values from -0.75 to 0.75
- source_index: int32 [64], replicated, may hold values from 0 to 5119, as said below
Outputs:
- correlation: float32 [4, 64, 5120, 512], P('tm', None, 'chan')
Inputs may be any that keep to these rules, and one draw needn't show every extreme that they name: `source_index`: the 64 channel numbers are distinct. They lie in 8 consecutive blocks of 80 channels (block b holding channels b * 80 to b * 80 + 79, counted around the fibre's end), at most 12 in one block, and exactly 12 in some block. Channels 0 and 5119 are always among them.
All inputs are finite; a program needn't handle non-finite values.
Results may differ from a plain program's by a relative error of at most 0.0029.
Values may be sent and summed in bfloat16 or wider, within the bound.
A program may use at most 192 MiB of HBM per device.

v0:
```python
import math

import jax
import jax.numpy as jnp
from jax import lax
from jax.sharding import Mesh
from jax.sharding import PartitionSpec as P

LAG_HALF = 256
NORM_HALF = 64
MAX_OWN = 12
CHAN = ("chan_0", "chan_1", "chan_2")


EPSILON = 1e-05


def extended_2(block, sides, width):
    for axis, dim in sides:
        count = lax.axis_size(axis)
        forward = [(i, i + 1) for i in range(count - 1)]
        backward = [(target, source) for source, target in forward]
        low = lax.ppermute(
            lax.slice_in_dim(block, block.shape[dim] - width, None, axis=dim), axis, forward
        )
        high = lax.ppermute(lax.slice_in_dim(block, 0, width, axis=dim), axis, backward)
        block = jnp.concatenate([low, block, high], axis=dim)
    return block


def joined_along(tiles, dim):
    shape = list(tiles.shape[1:])
    shape[dim] *= tiles.shape[0]
    return jnp.moveaxis(tiles, 0, dim).reshape(shape)


def all_blocks(x, axes, order):
    tiles = x[None]
    for k in order:
        tiles = lax.all_gather(tiles, axes[k], axis=0, tiled=True)
    carried = [lax.axis_size(axes[k]) for k in reversed(order)]
    tiles = tiles.reshape(*carried, *x.shape)
    turned = sorted(range(len(order)), key=lambda place: order[len(order) - 1 - place])
    return tiles.transpose(*turned, *range(len(order), tiles.ndim)).reshape(-1, *x.shape)


def whole_of(x, axes, order, dim):
    return joined_along(all_blocks(x, axes, order), dim)


def bandpass(padded, fir_taps):
    result = lax.conv_general_dilated(
        padded[:, None, :],
        fir_taps[None, None, :],
        (1,),
        "VALID",
        dimension_numbers=("NCH", "OIH", "NCH"),
        precision=lax.Precision.HIGHEST,
    )
    return result[:, 0, :]


def body(traces, fir_taps, source_index):
    channels, samples = traces.shape
    fir_half = (fir_taps.shape[0] - 1) // 2
    norm_half = NORM_HALF
    padded = extended_2(traces, (("tm", 1),), fir_half)
    filtered = bandpass(padded, fir_taps)
    filtered_wide = extended_2(filtered, (("tm", 1),), norm_half)
    window_sum = lax.reduce_window(
        jnp.abs(filtered_wide),
        jnp.zeros((), filtered_wide.dtype),
        lax.add,
        (1, 2 * norm_half + 1),
        (1, 1),
        "VALID",
    )
    normed = (filtered / (EPSILON + window_sum / (2 * norm_half + 1))).astype(jnp.bfloat16)
    own_block = lax.axis_index(CHAN)
    source_total = source_index.shape[0]
    owner = source_index // channels
    offset = source_index - owner * channels
    same_owner = owner[:, None] == owner[None, :]
    earlier = jnp.arange(source_total)[None, :] < jnp.arange(source_total)[:, None]
    rank = jnp.sum((same_owner & earlier).astype(jnp.int32), axis=1)
    slot_number = jnp.arange(MAX_OWN, dtype=jnp.int32)
    match = (owner[None, :] == own_block) & (rank[None, :] == slot_number[:, None])
    slot_offset = jnp.sum(jnp.where(match, offset[None, :], 0), axis=1)
    filled = jnp.any(match, axis=1)
    packed = jnp.where(
        filled[:, None], jnp.take(normed, slot_offset, axis=0), jnp.zeros((), jnp.bfloat16)
    )
    gathered = whole_of(packed, CHAN, (1, 0, 2), 0)
    sources = jnp.take(gathered, owner * MAX_OWN + rank, axis=0)
    lag_half = LAG_HALF
    extended = extended_2(sources, (("tm", 1),), lag_half)
    lag_width = min(128, 2 * lag_half)
    block_total = 2 * lag_half // lag_width
    shifted = jnp.pad(normed, ((0, 0), (lag_width, lag_width)))
    hankel = jnp.stack(
        [shifted[:, lag_width - j : lag_width - j + samples + lag_width] for j in range(lag_width)],
        axis=1,
    )
    windows = jnp.stack(
        [
            extended[:, i * lag_width : i * lag_width + samples + lag_width]
            for i in range(block_total)
        ],
        axis=0,
    )
    products = jnp.einsum("asu,cju->scaj", windows, hankel, preferred_element_type=jnp.float32)
    correlation = products.reshape(source_total, channels, 2 * lag_half) / math.sqrt(samples)
    return correlation[None]


def solution(mesh):
    torus = Mesh(
        mesh.devices.reshape(8, 4, 2, mesh.shape["tm"]), ("chan_0", "chan_1", "chan_2", "tm")
    )
    return jax.shard_map(
        body,
        mesh=torus,
        in_specs=(P(CHAN, "tm"), P(), P()),
        out_specs=P("tm", None, CHAN, None),
        check_vma=False,
    )
```

profile of v0, /device:TPU:1, one launch (start us, length us, event | category | flops | bytes accessed | tf_op | source)
XLA Modules:
  0.0 419.9 jit_solution(11522965348140188352)
XLA Ops:
  6.5 1.4 copy.45
  8.0 3.9 collective-permute-start
  11.9 1.3 collective-permute-start.1
  13.2 0.7 broadcast_compare_fusion
  14.1 0.7 multiply_subtract_fusion
  14.9 0.8 copy.48
  15.7 0.7 collective-permute-done.1
  16.5 158.8 %fusion.25 = f32[80,1,2048]{0,1,2:T(1,128)S(1)} fusion(f32[80,1,2112]{0,1,2:T(1,128)S(1)} %bitcast.298, f32[1,1,65]{1,0,2:T(1,128)S(1)} %copy.48), kind=kOutput, calls=%fused_computation.180 | convolution fusion | flops 127795200 | bytes 1331460 | tf_op jit(solution)/shard_map/conv_general_dilated | solution.py:52
  175.3 0.6 copy.49
  176.0 3.3 collective-permute-start.2
  179.2 1.5 collective-permute-start.3
  180.8 3.2 collective-permute-done.3
  184.4 37.1 %reduce_window.7 = f32[80,2048]{1,0:T(8,128)S(1)} reduce-window(f32[80,2176]{1,0:T(8,128)S(1)} %abs.3, f32[]{:T(128)} %constant.33.clone.1), window={size=1x129}, to_apply=%region_0.0 | reduce-window | flops 20971520 | bytes 1351684 | tf_op jit(solution)/shard_map/reduce_window | solution.py:70
  240.7 14.7 %copy-done = bf16[80,128,2176]{2,0,1:T(8,128)(2,1)} copy-done((bf16[80,128,2176]{2,0,1:T(8,128)(2,1)}, bf16[80,128,2176]{2,0,1:T(8,128)(2,1)S(1)}, u32[]{:S(2)}) %copy-start) | copy-done | bytes 44564504
  256.0 10.6 %all_gather.9 = bf16[4,12,2048]{2,1,0:T(8,128)(2,1)} all-gather(bf16[1,12,2048]{2,1,0:T(8,128)(2,1)S(1)} %fusion.16), channel_id=1, replica_groups=mesh['chan_0'=8,'chan_1'=4,'chan_2'=2,'tm'=4] {'chan_1'}, dimensions={0}, use_global_device_ids=true | all-gather | bytes 245760 | tf_op jit(solution)/shard_map/all_gather | solution.py:40
  267.0 0.9 bitcast_dynamic-update-slice_fusion.18
  267.9 0.9 bitcast_dynamic-update-slice_fusion.17
  268.8 0.9 bitcast_dynamic-update-slice_fusion.16
  269.7 0.9 bitcast_dynamic-update-slice_fusion.15
  270.6 0.9 bitcast_dynamic-update-slice_fusion.14
  271.5 0.9 bitcast_dynamic-update-slice_fusion.13
  272.4 0.9 bitcast_dynamic-update-slice_fusion.12
  273.4 0.9 bitcast_dynamic-update-slice_fusion.11
  274.3 36.1 %all-gather.3.cloned.1.call-done = bf16[32,12,2048]{2,1,0:T(8,128)(2,1)} async-done(((bf16[4,12,2048]{2,1,0:T(8,128)(2,1)}), bf16[32,12,2048]{2,1,0:T(8,128)(2,1)}) %all-gather.3.cloned.1.call-update) | async-done | bytes 1572880 | tf_op jit(solution)/shard_map/all_gather | solution.py:40
  310.4 3.6 copy.50
  314.0 0.9 bitcast_dynamic-update-slice_fusion.10
  314.9 0.9 bitcast_dynamic-update-slice_fusion.9
  315.8 0.9 bitcast_dynamic-update-slice_fusion.8
  316.7 0.9 bitcast_dynamic-update-slice_fusion.7
  317.6 0.9 bitcast_dynamic-update-slice_fusion.6
  318.5 0.9 bitcast_dynamic-update-slice_fusion.5
  319.4 0.9 bitcast_dynamic-update-slice_fusion.4
  320.3 0.9 bitcast_dynamic-update-slice_fusion.3
  321.2 0.9 bitcast_dynamic-update-slice_fusion.2
  322.2 0.9 bitcast_dynamic-update-slice_fusion.1
  323.1 12.0 %all-gather.5.cloned.1.call-done = bf16[64,12,2048]{2,0,1:T(8,128)(2,1)} async-done(((bf16[32,12,2048]{2,0,1:T(8,128)(2,1)}), bf16[64,12,2048]{2,0,1:T(8,128)(2,1)}) %all-gather.5.cloned.1.call-update) | async-done | bytes 3145744 | tf_op jit(solution)/shard_map/all_gather | solution.py:40
  335.1 4.0 reshape.89
  339.1 4.0 copy.55
  343.1 4.7 %reshape_reshape.3 = bf16[768,2048]{1,0:T(8,128)(2,1)S(1)} reshape(bf16[8,4,2,12,2048]{4,3,2,1,0:T(8,128)(2,1)} %bitcast.295) | data formatting | bytes 6291456 | tf_op jit(solution)/shard_map/reshape;reshape | solution.py:34
  347.8 1.4 gather_fusion.1
  349.2 1.0 broadcast_select_fusion
  350.3 2.8 collective-permute-start.4
  353.1 1.3 collective-permute-start.5
  354.4 0.9 bitcast_dynamic-update-slice_fusion
  355.3 2.5 collective-permute-done.5
  357.9 27.3 %multiply_bitcast_fusion = f32[64,80,4,128]{1,0,2,3:T(8,128)} fusion(bf16[80,128,2176]{2,0,1:T(8,128)(2,1)} %bitcast_dynamic-update-slice_fusion, bf16[1,64,2176]{2,1,0:T(8,128)(2,1)S(1)} %get-tuple-element.17, bf16[1,64,2176]{2,1,0:T(8,128)(2,1)S(1)} %get-tuple-element.18, bf16[1,64,2176]{2,1,0:T(8,128)(2,1)S(1)} %get-tuple-element.14, ...), kind=kOutput, calls=%fused_computation.4 | convolution fusion | flops 11415584768 | bytes 56164352 | tf_op jit(solution)/shard_map/asu,cju->scaj/dot_general | solution.py:111
  385.2 14.8 %copy.52 = f32[64,80,4,128]{3,2,1,0:T(4,128)} copy(f32[64,80,4,128]{1,0,2,3:T(8,128)} %multiply_bitcast_fusion) | data formatting | bytes 20971520 | tf_op jit(solution)/shard_map/div | solution.py:112
  400.0 12.7 %div.32 = f32[1,64,80,512]{3,2,1,0:T(8,128)} reshape(f32[64,80,4,128]{3,2,1,0:T(4,128)} %copy.52) | data formatting | bytes 20971520 | tf_op jit(solution)/shard_map/div | solution.py:112
  (134 shorter events, 21.0 us)
Async XLA Ops:
  6.5 303.8 %all-gather.3.cloned.1.call-start = ((), (), s32[]{:S(2)}) async-start(), calls=%async_computation | async-start | bytes 2359296 | tf_op jit(solution)/shard_map/all_gather | solution.py:40
  8.0 7.7 %collective-permute-start = (f32[80,32]{0,1:T(8,128)S(1)}, f32[80,32]{0,1:T(8,128)S(1)}, u32[]{:S(2)}, u32[]{:S(2)}) collective-permute-start(f32[80,32]{0,1:T(8,128)S(1)} %get-tuple-element.9), channel_id=1, source_target_pairs={{0,1},{1,2},{2,3},{4,5},{5,6},{6,7},{8,9},{9,10},{10,11},{12,13},{... | collective-permute-start | bytes 30728 | tf_op jit(solution)/shard_map/ppermute | solution.py:23
  11.9 4.5 %collective-permute-start.1 = (f32[80,32]{0,1:T(8,128)S(1)}, f32[80,32]{0,1:T(8,128)S(1)}, u32[]{:S(2)}, u32[]{:S(2)}) collective-permute-start(f32[80,32]{0,1:T(8,128)S(1)} %get-tuple-element.10), channel_id=1, source_target_pairs={{1,0},{2,1},{3,2},{5,4},{6,5},{7,6},{9,8},{10,9},{11,10},{13,12},{... | collective-permute-start | bytes 30728 | tf_op jit(solution)/shard_map/ppermute | solution.py:26
  176.0 4.9 %collective-permute-start.2 = (f32[80,64]{1,0:T(8,128)S(1)}, f32[80,64]{1,0:T(8,128)S(1)}, u32[]{:S(2)}, u32[]{:S(2)}) collective-permute-start(f32[80,64]{1,0:T(8,128)S(1)} %get-tuple-element.12), channel_id=1, source_target_pairs={{0,1},{1,2},{2,3},{4,5},{5,6},{6,7},{8,9},{9,10},{10,11},{12,13},{... | collective-permute-start | bytes 61448 | tf_op jit(solution)/shard_map/ppermute | solution.py:23
  179.2 4.7 %collective-permute-start.3 = (f32[80,64]{1,0:T(8,128)S(1)}, f32[80,64]{1,0:T(8,128)S(1)}, u32[]{:S(2)}, u32[]{:S(2)}) collective-permute-start(f32[80,64]{1,0:T(8,128)S(1)} %get-tuple-element.11), channel_id=1, source_target_pairs={{1,0},{2,1},{3,2},{5,4},{6,5},{7,6},{9,8},{10,9},{11,10},{13,12},{... | collective-permute-start | bytes 61448 | tf_op jit(solution)/shard_map/ppermute | solution.py:26
  240.7 14.7 %copy-start = (bf16[80,128,2176]{2,0,1:T(8,128)(2,1)}, bf16[80,128,2176]{2,0,1:T(8,128)(2,1)S(1)}, u32[]{:S(2)}) copy-start(bf16[80,128,2176]{2,0,1:T(8,128)(2,1)S(1)} %bitcast_dynamic-update-slice_fusion.19) | copy-start | bytes 133693440
  266.7 68.4 %all-gather.5.cloned.1.call-start = ((), (), s32[]{:S(2)}) async-start(), calls=%async_computation.1 | async-start | bytes 4718592 | tf_op jit(solution)/shard_map/all_gather | solution.py:40
  350.3 5.0 %collective-permute-start.4 = (bf16[64,256]{1,0:T(8,128)(2,1)S(1)}, bf16[64,256]{1,0:T(8,128)(2,1)S(1)}, u32[]{:S(2)}, u32[]{:S(2)}) collective-permute-start(bf16[64,256]{1,0:T(8,128)(2,1)S(1)} %get-tuple-element.19), channel_id=1, source_target_pairs={{0,1},{1,2},{2,3},{4,5},{5,6},{6,7},{8,9},{9,10},{10,11},{12,13},{... | collective-permute-start | bytes 98312 | tf_op jit(solution)/shard_map/ppermute | solution.py:23
  353.1 4.7 %collective-permute-start.5 = (bf16[64,256]{1,0:T(8,128)(2,1)S(1)}, bf16[64,256]{1,0:T(8,128)(2,1)S(1)}, u32[]{:S(2)}, u32[]{:S(2)}) collective-permute-start(bf16[64,256]{1,0:T(8,128)(2,1)S(1)} %get-tuple-element.20), channel_id=1, source_target_pairs={{1,0},{2,1},{3,2},{5,4},{6,5},{7,6},{9,8},{10,9},{11,10},{13,12},{... | collective-permute-start | bytes 98312 | tf_op jit(solution)/shard_map/ppermute | solution.py:26
Sparse Core Ops, SparseCore 0:
  266.8 43.5 all-gather.2
  314.1 20.9 all-gather.4
where the time goes:
time: 428 us; the launch traced here: 420 us
  matrix products  186 us (43%)
  local copies, waits for them, and re-layouts  99.7 us (23%)
  waiting for transfers between devices  54.5 us (13%)
  other arithmetic  40.4 us (9%)
  starting transfers between devices  14.4 us (3%)
  between operations  14.3 us (3%)
  blocking collectives  10.6 us (2%)
    conv_general_dilated x1, matrix products, bandpass(): lax.conv_general_dilated(padded[:, None, :], fir_taps[None, None, :], (1,...  159 us
    unnamed x130, local copies, waits for them, and re-layouts  51.2 us
    all_gather x2, waiting for transfers between devices, all_blocks(): tiles = lax.all_gather(tiles, axes[k], axis=0, tiled=True)  48.2 us
    another operation x1, other arithmetic, body(): lax.reduce_window(jnp.abs(filtered_wide), jnp.zeros((), filtered_wide.dty...  37.1 us
    div x2, local copies, waits for them, and re-layouts, body(): products.reshape(source_total, channels, 2 * lag_half) / math.sqrt(samples)  27.5 us
    dot_general x1, matrix products, body(): jnp.einsum('asu,cju->scaj', windows, hankel, preferred_element_type=jnp.f...  27.3 us
    all_gather x1, blocking collectives, all_blocks(): tiles = lax.all_gather(tiles, axes[k], axis=0, tiled=True)  10.6 us
    ppermute x3, starting transfers between devices, extended_2(): lax.ppermute(lax.slice_in_dim(block, block.shape[dim] - width, None, axis...  10 us
  transfers between devices with their start and end apart: 8, of which 5 were waited for; matrix products, arithmetic and copies ran while one was open for 5% of the time, Pallas kernels for 0%

commit v1 on v0

v1 whole, which is shorter than its diff:
```python
import math

import jax
import jax.numpy as jnp
from jax import lax
from jax.experimental import pallas as pl
from jax.experimental.pallas import tpu as pltpu
from jax.sharding import Mesh
from jax.sharding import PartitionSpec as P

CHN, T, S = 80, 2048, 64
EPSILON = 1e-05
FIR_HALF, NORM_HALF, LAG_HALF = 32, 64, 256
TAPS = 2 * FIR_HALF + 1
SLOTS = 12
NB = T // 128
NP = T // 256
K = T + 128
AXES = ("chan_0", "chan_1", "chan_2", "tm")
NZ, NY, NC, NX = 8, 4, 2, 4
CHUNKS = ((0, 48), (48, 48), (96, 32))
UP = (True, False, True)
ROWS = 128
BF = jnp.bfloat16
F32 = jnp.float32


def dot(a, b):
    return jnp.dot(a, b, preferred_element_type=F32)


def dot_t(a, b):
    return lax.dot_general(a, b, (((1,), (1,)), ((), ())), preferred_element_type=F32)


def iota(shape, dim):
    return lax.broadcasted_iota(jnp.int32, shape, dim)


def gather_kernel(
    traces, fir, index, src_out, nr_out,
    xbuf, halo, xh, xl, band, fbuf, fa, fb, nb, nrev, pick, edge, pack, zu, zd, gath, unp,
    lsem, hsem, esem, zsem, ysem, csem,
):
    z, y, core, x = (lax.axis_index(a) for a in AXES)
    up_z = {"chan_0": lax.rem(z + 1, NZ)}
    dn_z = {"chan_0": lax.rem(z + NZ - 1, NZ)}
    up_y = {"chan_1": lax.rem(y + 1, NY)}
    dn_y = {"chan_1": lax.rem(y + NY - 1, NY)}
    other = {"chan_2": 1 - core}
    right = {"tm": lax.rem(x + 1, NX)}
    left = {"tm": lax.rem(x + NX - 1, NX)}

    load = pltpu.make_async_copy(traces, xbuf, lsem.at[0])
    load.start()
    barrier = pltpu.get_barrier_semaphore()
    peers = (up_z, dn_z, up_y, dn_y, other, right, left)
    for peer in peers:
        pl.semaphore_signal(barrier, inc=1, device_id=peer, device_id_type=pl.DeviceIdType.MESH)
    pl.semaphore_wait(barrier, len(peers))

    def remote(src, dst, sems, peer):
        return pltpu.make_async_remote_copy(
            src_ref=src, dst_ref=dst, send_sem=sems.at[0], recv_sem=sems.at[1],
            device_id=peer, device_id_type=pl.DeviceIdType.MESH,
        )

    to_right = remote(traces.at[:, T - 128:T], halo.at[0], hsem.at[0], right)
    to_left = remote(traces.at[:, 0:128], halo.at[1], hsem.at[1], left)
    to_right.start()
    to_left.start()

    lane = iota((8, 128), 1)
    taps = jnp.zeros((8, 128), F32)
    for k in range(TAPS):
        taps = jnp.where(lane == k, fir[k], taps)
    rolled = pltpu.roll(jnp.concatenate([taps] * 16, axis=0), 128 - FIR_HALF, 1, stride=1, stride_axis=0)
    apart = iota((128, 128), 1) - iota((128, 128), 0)
    zero = jnp.zeros((128, 128), F32)
    d1 = jnp.where(apart >= 128 - FIR_HALF, rolled, zero)
    d2 = jnp.where(jnp.abs(apart) <= FIR_HALF, rolled, zero)
    d3 = jnp.where(apart <= FIR_HALF - 128, rolled, zero)
    for n, blocks in enumerate((((d1, d2), (zero, d1)), ((d3, zero), (d2, d3)))):
        for i in range(2):
            for u in range(2):
                whole = blocks[i][u]
                high = whole.astype(BF)
                at = (slice(i * 128, i * 128 + 128), slice(u * 128, u * 128 + 128))
                band[(2 * n,) + at] = high
                band[(2 * n + 1,) + at] = (whole - high.astype(F32)).astype(BF)
    gap = iota((256, 256), 0) - iota((256, 256), 1)
    one = jnp.ones((256, 256), F32)
    none = jnp.zeros((256, 256), F32)
    band[4] = jnp.where((gap >= NORM_HALF) & (gap <= 3 * NORM_HALF), one, none).astype(BF)
    band[5] = jnp.where((gap <= -NORM_HALF) & (gap >= -3 * NORM_HALF), one, none).astype(BF)
    band[6] = jnp.where(iota((256, 256), 0) + iota((256, 256), 1) == 255, one, none).astype(BF)

    own = (z * NY + y) * NC + core
    lanes = iota((128, 128), 1)
    subs = iota((128, 128), 0)
    row = jnp.full((8, 128), -1, jnp.int32)
    for s in range(S):
        row = jnp.where(lane == s, index[s], row)
    rows = jnp.concatenate([row] * 16, axis=0)
    inside = (rows >= own * CHN) & (rows < own * CHN + CHN)
    fone, fnone = jnp.ones((128, 128), F32), jnp.zeros((128, 128), F32)
    mine = jnp.where(inside, fone, fnone)
    before = jnp.where(subs < lanes, fone, fnone)
    rank = dot(mine.astype(BF), before.astype(BF))
    hit = jnp.where(inside & (rows == own * CHN + subs), fone, fnone).astype(BF)[0:CHN]
    subf = subs.astype(F32)
    for i in range(4):
        slot = jnp.where(inside & (subf == rank + SLOTS * i), fone, fnone).astype(BF)[0:48]
        pick[i] = dot_t(slot, hit).astype(BF)

    colsum = jnp.sum(jnp.where(subs == lanes, rows.astype(F32), fnone), axis=1, keepdims=True)
    owner_col = jnp.floor((colsum + 0.5) * (1.0 / CHN))
    owner_row = jnp.floor((rows.astype(F32) + 0.5) * (1.0 / CHN))
    rank_col = jnp.sum(
        jnp.where((owner_row == owner_col) & (lanes < subs), fone, fnone), axis=1, keepdims=True
    )
    residue = owner_col - 8.0 * jnp.floor(owner_col * 0.125)
    place = (residue * ROWS + rank_col)[0:S]
    wide = iota((S, 8 * ROWS), 1).astype(F32)
    uone, unone = jnp.ones((S, 8 * ROWS), F32), jnp.zeros((S, 8 * ROWS), F32)
    for e in range(NP + 2):
        offset = 96 if e == 0 else 112 if e == NP + 1 else SLOTS * (e - 1)
        unp[e * S:(e + 1) * S, :] = jnp.where(wide == place + offset, uone, unone).astype(BF)

    def put(group, half, block):
        high = block.astype(BF)
        at = (slice(group * CHN, group * CHN + CHN), slice(half * 128, half * 128 + 128))
        xh[at] = high
        xl[at] = (block - high.astype(F32)).astype(BF)

    load.wait()
    for b in range(NB):
        put(1 + b // 2, b % 2, xbuf[:, b * 128:b * 128 + 128])
    nothing = jnp.zeros((CHN, 128), F32)
    put(0, 0, nothing)
    put(NP + 1, 1, nothing)

    def filtered(lo, hi):
        n = slice(lo * CHN, hi * CHN)
        m = slice((lo + 1) * CHN, (hi + 1) * CHN)
        value = dot_t(xh[n], band[0]) + dot_t(xh[m], band[2])
        value += dot_t(xl[n], band[0]) + dot_t(xl[m], band[2])
        value += dot_t(xh[n], band[1]) + dot_t(xh[m], band[3])
        return value

    def keep(lo, hi, value):
        n = slice(lo * CHN, hi * CHN)
        fbuf[n] = value
        size = jnp.abs(value)
        high = size.astype(BF)
        fa[n] = high
        fb[n] = (size - high.astype(F32)).astype(BF)

    keep(1, NP, filtered(1, NP))
    to_right.wait_recv()
    to_left.wait_recv()
    put(0, 1, jnp.where(x > 0, halo[0], nothing))
    put(NP + 1, 0, jnp.where(x < NX - 1, halo[1], nothing))
    ends = iota((CHN, 256), 1)
    empty = jnp.zeros((CHN, 256), F32)
    keep(0, 1, jnp.where((ends >= 128) | (x > 0), filtered(0, 1), empty))
    keep(NP, NP + 1, jnp.where((ends < 128) | (x < NX - 1), filtered(NP, NP + 1), empty))

    first, second = slice(0, NP * CHN), slice(CHN, (NP + 1) * CHN)
    level = dot(fa[first], band[4]) + dot(fa[second], band[5])
    level += dot(fb[first], band[4]) + dot(fb[second], band[5])
    below = EPSILON + level / (2 * NORM_HALF + 1)
    nb[:, 0:128] = (fbuf[first, 128:256] / below[:, 0:128]).astype(BF)
    nb[:, 128:256] = (fbuf[second, 0:128] / below[:, 128:256]).astype(BF)

    def pair(p):
        return nb[p * CHN:(p + 1) * CHN]

    lower = dot(pick[0], pair(0))[0:16]
    upper = dot(pick[0], pair(NP - 1))[0:16]
    edge[0] = jnp.where(x > 0, lower, jnp.zeros_like(lower)).astype(BF)
    edge[1] = jnp.where(x < NX - 1, upper, jnp.zeros_like(upper)).astype(BF)
    for j in range(2):
        total = dot(pick[0], pair(4 * j))
        for i in range(1, 4):
            total += dot(pick[i], pair(4 * j + i))
        pack[48 * j:48 * j + 48, :] = total.astype(BF)

    edge_left = remote(edge.at[0], pack.at[112:128], esem.at[0], left)
    edge_right = remote(edge.at[1], pack.at[96:112], esem.at[1], right)
    edge_left.start()
    edge_right.start()

    def part(ref, k):
        at, size = CHUNKS[k]
        return ref.at[at:at + size]

    def ring(direction, hop, k):
        slots, peer = (zu, up_z) if direction == 0 else (zd, dn_z)
        src = part(pack, k) if hop == 0 else part(slots.at[hop - 1], k)
        return remote(src, part(slots.at[hop], k), zsem.at[direction, hop, k], peer)

    def rings(hop, k):
        return [d for d in range(2) if hop < 3 or (d == 0) == UP[k]]

    started = [to_right, to_left, edge_left, edge_right]

    def go(copy):
        copy.start()
        started.append(copy)

    for k in range(2):
        for d in rings(0, k):
            go(ring(d, 0, k))
    edge_left.wait_recv()
    edge_right.wait_recv()
    for d in rings(0, 2):
        go(ring(d, 0, 2))

    turned = dot(nb[...], band[6])
    for p in range(NP):
        for h in range(2):
            nrev[(NP - 1 - p) * 2 + h] = turned[p * CHN:(p + 1) * CHN, h * 128:h * 128 + 128]
    save = pltpu.make_async_copy(nrev, nr_out, lsem.at[1])
    save.start()

    for hop in range(1, 4):
        for k in range(3):
            for d in range(2):
                ring(d, hop - 1, k).wait_recv()
                if d in rings(hop, k):
                    go(ring(d, hop, k))

    me = y * NC + core

    def hold(slot, k):
        at, size = CHUNKS[k]
        return gath.at[slot, at:at + size]

    low, high = lax.rem(y + NY - 1, NY) * NC + core, lax.rem(y + 1, NY) * NC + core
    far = lax.rem(y + 2, NY) * NC + core
    origin = (me, low, high, far)

    def line(kind, k):
        if kind == 0:
            slot, peer = me, up_y
        elif kind == 1:
            slot, peer = me, dn_y
        else:
            slot, peer = (low, up_y) if UP[k] else (high, dn_y)
        return remote(hold(slot, k), hold(slot, k), ysem.at[kind, k], peer)

    def across(n, k):
        return remote(hold(origin[n], k), hold(origin[n], k), csem.at[n, k], other)

    for k in range(3):
        at, size = CHUNKS[k]
        for d in rings(3, k):
            ring(d, 3, k).wait_recv()
        total = pack[at:at + size]
        for hop in range(3):
            total += zu[hop, at:at + size] + zd[hop, at:at + size]
        total += (zu if UP[k] else zd)[3, at:at + size]
        gath[me, at:at + size] = total
        go(line(0, k))
        go(line(1, k))
        go(across(0, k))
    for k in range(3):
        line(0, k).wait_recv()
        if UP[k]:
            go(line(2, k))
        go(across(1, k))
        line(1, k).wait_recv()
        if not UP[k]:
            go(line(2, k))
        go(across(2, k))
    for k in range(3):
        line(2, k).wait_recv()
        go(across(3, k))
    for n in range(4):
        for k in range(3):
            across(n, k).wait_recv()

    spread = dot(unp[...], gath[...].reshape(8 * ROWS, 256)).astype(BF)
    for e in range(NP + 2):
        src_out[:, e * 256:(e + 1) * 256] = spread[e * S:(e + 1) * S]
    for copy in started:
        copy.wait_send()
    save.wait()


def gather(traces, fir, index):
    dma = pltpu.SemaphoreType.DMA
    return pl.pallas_call(
        gather_kernel,
        in_specs=[
            pl.BlockSpec(memory_space=pl.ANY),
            pl.BlockSpec(memory_space=pltpu.SMEM),
            pl.BlockSpec(memory_space=pltpu.SMEM),
        ],
        out_specs=[pl.BlockSpec(memory_space=pltpu.VMEM), pl.BlockSpec(memory_space=pl.ANY)],
        out_shape=[
            jax.ShapeDtypeStruct((S, T + 2 * LAG_HALF), BF),
            jax.ShapeDtypeStruct((NB, CHN, 128), F32),
        ],
        scratch_shapes=[
            pltpu.VMEM((CHN, T), F32),
            pltpu.VMEM((2, CHN, 128), F32),
            pltpu.VMEM(((NP + 2) * CHN, 256), BF),
            pltpu.VMEM(((NP + 2) * CHN, 256), BF),
            pltpu.VMEM((7, 256, 256), BF),
            pltpu.VMEM(((NP + 1) * CHN, 256), F32),
            pltpu.VMEM(((NP + 1) * CHN, 256), BF),
            pltpu.VMEM(((NP + 1) * CHN, 256), BF),
            pltpu.VMEM((NP * CHN, 256), BF),
            pltpu.VMEM((NB, CHN, 128), F32),
            pltpu.VMEM((4, 48, CHN), BF),
            pltpu.VMEM((2, 16, 256), BF),
            pltpu.VMEM((ROWS, 256), BF),
            pltpu.VMEM((4, ROWS, 256), BF),
            pltpu.VMEM((4, ROWS, 256), BF),
            pltpu.VMEM((8, ROWS, 256), BF),
            pltpu.VMEM(((NP + 2) * S, 8 * ROWS), BF),
            dma((2,)),
            dma((2, 2)),
            dma((2, 2)),
            dma((2, 4, 3, 2)),
            dma((3, 3, 2)),
            dma((4, 3, 2)),
        ],
        compiler_params=pltpu.CompilerParams(
            collective_id=0, has_side_effects=True, vmem_limit_bytes=40 << 20
        ),
        name="gather",
    )(traces, fir, index)


def corr_kernel(src_ref, nr_ref, o_ref, w_ref, h0, h1):
    g = pl.program_id(0)
    keep = iota((128, 128), 1) > iota((128, 128), 0)

    def build(h, c, half):
        cols = slice(half * 128, half * 128 + 128)
        prev = jnp.zeros((128, 128), F32)
        for q in range(NB + 1):
            b = NB - q
            if b >= 1:
                x = nr_ref.at[b - 1][pl.ds(c, 128, stride=0), :]
                cur = pltpu.roll(x, 1, 1, stride=1, stride_axis=0)
            else:
                cur = jnp.zeros((128, 128), F32)
            h[q * 128:(q + 1) * 128, cols] = jnp.where(keep, prev, cur).astype(BF)
            prev = cur

    @pl.when(g == 0)
    def _():
        for a in range(4):
            w_ref[a * S:(a + 1) * S, :] = src_ref[:, a * 128:a * 128 + K]
        build(h0, 0, 0)
        build(h0, 1, 1)

    out2 = o_ref.reshape(S * 4 * 8, 128)
    bufs = (h0, h1)
    for p in range(4):
        nxt = lax.rem(g * 8 + 2 * p + 2, CHN)
        build(bufs[(p + 1) % 2], nxt, 0)
        build(bufs[(p + 1) % 2], nxt + 1, 1)
        res = dot(w_ref[...], bufs[p % 2][...]) * (1.0 / math.sqrt(T))
        for a in range(4):
            for hh in range(2):
                out2[pl.ds(a * 8 + 2 * p + hh, S, stride=32), :] = res[
                    a * S:(a + 1) * S, hh * 128:hh * 128 + 128
                ]


def corr(src_ext, nr):
    out = pl.pallas_call(
        corr_kernel,
        grid=(CHN // 8,),
        in_specs=[
            pl.BlockSpec((S, T + 2 * LAG_HALF), lambda g: (0, 0)),
            pl.BlockSpec((NB, CHN, 128), lambda g: (0, 0, 0)),
        ],
        out_specs=pl.BlockSpec((S, 1, 4, 8, 128), lambda g: (0, g, 0, 0, 0)),
        out_shape=jax.ShapeDtypeStruct((S, CHN // 8, 4, 8, 128), F32),
        scratch_shapes=[
            pltpu.VMEM((4 * S, K), BF),
            pltpu.VMEM((K, 256), BF),
            pltpu.VMEM((K, 256), BF),
        ],
        compiler_params=pltpu.CompilerParams(
            dimension_semantics=("arbitrary",), vmem_limit_bytes=60 << 20
        ),
        name="corr",
    )(src_ext, nr)
    return out.transpose(0, 1, 3, 2, 4).reshape(S, CHN, 2 * LAG_HALF)


def body(traces, fir_taps, source_index):
    src_ext, nr = gather(traces, fir_taps, source_index)
    return corr(src_ext, nr)[None]


def solution(mesh):
    torus = Mesh(mesh.devices.reshape(NZ, NY, NC, NX), AXES)
    chan = AXES[:3]
    return jax.shard_map(
        body,
        mesh=torus,
        in_specs=(P(chan, "tm"), P(), P()),
        out_specs=P("tm", None, chan, None),
        check_vma=False,
    )
```

time: 428 us -> 68.6 us (0.16); the launches traced: 420 us -> 68.4 us
  matrix products: 186 us -> 0 us
  local copies, waits for them, and re-layouts: 99.7 us -> 3.95 us
  Pallas kernels: 0 us -> 64.5 us
  waiting for transfers between devices: 54.5 us -> 0 us
  other arithmetic: 40.4 us -> 0 us
  starting transfers between devices: 14.4 us -> 0 us
  between operations: 14.3 us -> 0.02 us
  blocking collectives: 10.6 us -> 0 us
    conv_general_dilated x1 -> x0, matrix products: 159 us -> none  [bandpass(): lax.conv_general_dilated(padded[:, None, :], fir_taps[None, None, :], (1,...]
    pallas_call x0 -> x2, Pallas kernels: none -> 64.5 us  [the longest x1 39.4 us: gather(): pl.pallas_call(gather_kernel, in_specs=[pl.BlockSpec(memory_space=pl.ANY)...]
    all_gather x2 -> x0, waiting for transfers between devices: 48.2 us -> none  [all_blocks(): tiles = lax.all_gather(tiles, axes[k], axis=0, tiled=True)]
    unnamed x130 -> x10, local copies, waits for them, and re-layouts: 51.2 us -> 3.95 us
    another operation x2 -> x0, other arithmetic: 37.2 us -> none  [the longest x1 37.1 us: body(): lax.reduce_window(jnp.abs(filtered_wide), jnp.zeros((), filtered_wide.dty...]
    div x2 -> x0, local copies, waits for them, and re-layouts: 27.5 us -> none  [body(): products.reshape(source_total, channels, 2 * lag_half) / math.sqrt(samples)]
    dot_general x1 -> x0, matrix products: 27.3 us -> none  [body(): jnp.einsum('asu,cju->scaj', windows, hankel, preferred_element_type=jnp.f...]
    ppermute x6 -> x0, starting transfers between devices: 14.1 us -> none  [the longest x3 10 us: extended_2(): lax.ppermute(lax.slice_in_dim(block, block.shape[dim] - width, None, axis...]
  transfers between devices with their start and end apart: 8 -> 0, of which waited for: 5 -> 0; matrix products, arithmetic and copies ran while one was open for 5% -> 0% of each run, Pallas kernels for 0% -> 0%
where the time goes in v1:
time: 68.6 us; the launch traced here: 68.4 us
  Pallas kernels  64.5 us (94%)
  local copies, waits for them, and re-layouts  3.95 us (6%)
    pallas_call x1, Pallas kernels, gather(): pl.pallas_call(gather_kernel, in_specs=[pl.BlockSpec(memory_space=pl.ANY)...  39.4 us
    pallas_call x1, Pallas kernels, corr(): pl.pallas_call(corr_kernel, grid=(CHN // 8,), in_specs=[pl.BlockSpec((S,...  25.1 us
    unnamed x10, local copies, waits for them, and re-layouts  3.95 us

profile of v1, /device:TPU:1, one launch (start us, length us, event | category | flops | bytes accessed | tf_op | source)
XLA Modules:
  0.0 68.4 jit_solution(12512238268154063337)
XLA Ops:
  0.0 0.0 copy-start.1
  0.0 1.1 %copy-done.1 = f32[80,2048]{1,0:T(8,128)S(1)} copy-done((f32[80,2048]{1,0:T(8,128)S(1)}, f32[80,2048]{1,0:T(8,128)}, u32[]{:S(2)}) %copy-start.1) | copy-done | bytes 655384
  1.1 0.0 copy-start.3
  1.1 0.7 copy-done.3
  1.7 0.0 copy-start.4
  1.7 0.7 copy-done.4
  2.4 39.4 %gather.1 = (bf16[64,2560]{1,0:T(8,128)(2,1)S(1)}, f32[16,80,128]{2,1,0:T(8,128)S(1)}) custom-call(f32[80,2048]{1,0:T(8,128)S(1)} %copy-done.1, f32[65]{0:T(128)S(1)} %copy-done.3, s32[64]{0:T(128)S(1)} %copy-done.4), custom_call_target="tpu_custom_call" | custom-call | tf_op jit(solution)/shard_map/gather/pallas_call | solution.py:294
  41.8 0.0 copy-start
  41.8 0.8 %copy-done = f32[16,80,128]{2,1,0:T(8,128)} copy-done((f32[16,80,128]{2,1,0:T(8,128)}, f32[16,80,128]{2,1,0:T(8,128)S(1)}, u32[]{:S(2)}) %copy-start) | copy-done | bytes 655384
  42.6 0.0 copy-start.2
  42.6 0.7 %copy-done.2 = bf16[64,2560]{1,0:T(8,128)(2,1)} copy-done((bf16[64,2560]{1,0:T(8,128)(2,1)}, bf16[64,2560]{1,0:T(8,128)(2,1)S(1)}, u32[]{:S(2)}) %copy-start.2) | copy-done | bytes 327704
  43.3 25.1 %corr.1 = f32[64,10,4,8,128]{4,3,2,1,0:T(8,128)} custom-call(bf16[64,2560]{1,0:T(8,128)(2,1)} %copy-done.2, f32[16,80,128]{2,1,0:T(8,128)} %copy-done), custom_call_target="tpu_custom_call" | custom-call | tf_op jit(solution)/shard_map/corr/pallas_call | solution.py:377
Async XLA Ops:
  0.0 1.1 %copy-start.1 = (f32[80,2048]{1,0:T(8,128)S(1)}, f32[80,2048]{1,0:T(8,128)}, u32[]{:S(2)}) copy-start(f32[80,2048]{1,0:T(8,128)} %traces.1) | copy-start | bytes 1966084
  1.1 0.7 copy-start.3
  1.7 0.7 copy-start.4
  41.8 0.8 %copy-start = (f32[16,80,128]{2,1,0:T(8,128)}, f32[16,80,128]{2,1,0:T(8,128)S(1)}, u32[]{:S(2)}) copy-start(f32[16,80,128]{2,1,0:T(8,128)S(1)} %get-tuple-element.8.nr_ref) | copy-start | bytes 1966084
  42.6 0.7 %copy-start.2 = (bf16[64,2560]{1,0:T(8,128)(2,1)}, bf16[64,2560]{1,0:T(8,128)(2,1)S(1)}, u32[]{:S(2)}) copy-start(bf16[64,2560]{1,0:T(8,128)(2,1)S(1)} %get-tuple-element.7.src_ref) | copy-start | bytes 983044

commit v2 on v1

--- a/solution.py
+++ b/solution.py
@@ -21,6 +21,7 @@
 CHUNKS = ((0, 48), (48, 48), (96, 32))
 UP = (True, False, True)
 ROWS = 128
+ORDER = (1, 2, 3, 4, 5, 6, 0, 7)
 BF = jnp.bfloat16
 F32 = jnp.float32
 
@@ -45,8 +46,11 @@
     z, y, core, x = (lax.axis_index(a) for a in AXES)
     up_z = {"chan_0": lax.rem(z + 1, NZ)}
     dn_z = {"chan_0": lax.rem(z + NZ - 1, NZ)}
+    up2_z = {"chan_0": lax.rem(z + 2, NZ)}
+    dn2_z = {"chan_0": lax.rem(z + NZ - 2, NZ)}
     up_y = {"chan_1": lax.rem(y + 1, NY)}
     dn_y = {"chan_1": lax.rem(y + NY - 1, NY)}
+    far_y = {"chan_1": lax.rem(y + 2, NY)}
     other = {"chan_2": 1 - core}
     right = {"tm": lax.rem(x + 1, NX)}
     left = {"tm": lax.rem(x + NX - 1, NX)}
@@ -54,7 +58,7 @@
     load = pltpu.make_async_copy(traces, xbuf, lsem.at[0])
     load.start()
     barrier = pltpu.get_barrier_semaphore()
-    peers = (up_z, dn_z, up_y, dn_y, other, right, left)
+    peers = (up2_z, dn2_z, up_z, dn_z, far_y, up_y, dn_y, other, right, left)
     for peer in peers:
         pl.semaphore_signal(barrier, inc=1, device_id=peer, device_id_type=pl.DeviceIdType.MESH)
     pl.semaphore_wait(barrier, len(peers))
@@ -124,7 +128,7 @@
     wide = iota((S, 8 * ROWS), 1).astype(F32)
     uone, unone = jnp.ones((S, 8 * ROWS), F32), jnp.zeros((S, 8 * ROWS), F32)
     for e in range(NP + 2):
-        offset = 96 if e == 0 else 112 if e == NP + 1 else SLOTS * (e - 1)
+        offset = 96 if e == 0 else 112 if e == NP + 1 else SLOTS * ORDER.index(e - 1)
         unp[e * S:(e + 1) * S, :] = jnp.where(wide == place + offset, uone, unone).astype(BF)
 
     def put(group, half, block):
@@ -156,7 +160,51 @@
         fa[n] = high
         fb[n] = (size - high.astype(F32)).astype(BF)
 
+    def normalize(lo, hi):
+        first, second = slice(lo * CHN, hi * CHN), slice((lo + 1) * CHN, (hi + 1) * CHN)
+        level = dot(fa[first], band[4]) + dot(fa[second], band[5])
+        level += dot(fb[first], band[4]) + dot(fb[second], band[5])
+        below = EPSILON + level / (2 * NORM_HALF + 1)
+        nb[first, 0:128] = (fbuf[first, 128:256] / below[:, 0:128]).astype(BF)
+        nb[first, 128:256] = (fbuf[second, 0:128] / below[:, 128:256]).astype(BF)
+
+    def pair(p):
+        return nb[p * CHN:(p + 1) * CHN]
+
+    def fold(j):
+        total = dot(pick[0], pair(ORDER[4 * j]))
+        for i in range(1, 4):
+            total += dot(pick[i], pair(ORDER[4 * j + i]))
+        pack[48 * j:48 * j + 48, :] = total.astype(BF)
+
+    def part(ref, k):
+        at, size = CHUNKS[k]
+        return ref.at[at:at + size]
+
+    def ring(d, far, k):
+        slots, two, near = (zu, up2_z, up_z) if d == 0 else (zd, dn2_z, dn_z)
+        src = part(pack, k) if far < 2 else part(slots.at[1], k)
+        peer = (near, two, near, two)[far]
+        return remote(src, part(slots.at[far], k), zsem.at[d, far, k], peer)
+
+    def rings(far, k):
+        return [d for d in range(2) if far < 3 or (d == 0) == UP[k]]
+
+    started = [to_right, to_left]
+
+    def go(copy):
+        copy.start()
+        started.append(copy)
+
+    def send(k):
+        for far in (1, 0):
+            for d in range(2):
+                go(ring(d, far, k))
+
     keep(1, NP, filtered(1, NP))
+    normalize(1, NP - 1)
+    fold(0)
+    send(0)
     to_right.wait_recv()
     to_left.wait_recv()
     put(0, 1, jnp.where(x > 0, halo[0], nothing))
@@ -165,58 +213,19 @@
     empty = jnp.zeros((CHN, 256), F32)
     keep(0, 1, jnp.where((ends >= 128) | (x > 0), filtered(0, 1), empty))
     keep(NP, NP + 1, jnp.where((ends < 128) | (x < NX - 1), filtered(NP, NP + 1), empty))
-
-    first, second = slice(0, NP * CHN), slice(CHN, (NP + 1) * CHN)
-    level = dot(fa[first], band[4]) + dot(fa[second], band[5])
-    level += dot(fb[first], band[4]) + dot(fb[second], band[5])
-    below = EPSILON + level / (2 * NORM_HALF + 1)
-    nb[:, 0:128] = (fbuf[first, 128:256] / below[:, 0:128]).astype(BF)
-    nb[:, 128:256] = (fbuf[second, 0:128] / below[:, 128:256]).astype(BF)
-
-    def pair(p):
-        return nb[p * CHN:(p + 1) * CHN]
-
+    normalize(0, 1)
+    normalize(NP - 1, NP)
     lower = dot(pick[0], pair(0))[0:16]
     upper = dot(pick[0], pair(NP - 1))[0:16]
     edge[0] = jnp.where(x > 0, lower, jnp.zeros_like(lower)).astype(BF)
     edge[1] = jnp.where(x < NX - 1, upper, jnp.zeros_like(upper)).astype(BF)
-    for j in range(2):
-        total = dot(pick[0], pair(4 * j))
-        for i in range(1, 4):
-            total += dot(pick[i], pair(4 * j + i))
-        pack[48 * j:48 * j + 48, :] = total.astype(BF)
 
     edge_left = remote(edge.at[0], pack.at[112:128], esem.at[0], left)
     edge_right = remote(edge.at[1], pack.at[96:112], esem.at[1], right)
-    edge_left.start()
-    edge_right.start()
-
-    def part(ref, k):
-        at, size = CHUNKS[k]
-        return ref.at[at:at + size]
-
-    def ring(direction, hop, k):
-        slots, peer = (zu, up_z) if direction == 0 else (zd, dn_z)
-        src = part(pack, k) if hop == 0 else part(slots.at[hop - 1], k)
-        return remote(src, part(slots.at[hop], k), zsem.at[direction, hop, k], peer)
-
-    def rings(hop, k):
-        return [d for d in range(2) if hop < 3 or (d == 0) == UP[k]]
-
-    started = [to_right, to_left, edge_left, edge_right]
-
-    def go(copy):
-        copy.start()
-        started.append(copy)
-
-    for k in range(2):
-        for d in rings(0, k):
-            go(ring(d, 0, k))
-    edge_left.wait_recv()
-    edge_right.wait_recv()
-    for d in rings(0, 2):
-        go(ring(d, 0, 2))
-
+    go(edge_left)
+    go(edge_right)
+    fold(1)
+    send(1)
     turned = dot(nb[...], band[6])
     for p in range(NP):
         for h in range(2):
@@ -224,12 +233,19 @@
     save = pltpu.make_async_copy(nrev, nr_out, lsem.at[1])
     save.start()
 
-    for hop in range(1, 4):
-        for k in range(3):
-            for d in range(2):
-                ring(d, hop - 1, k).wait_recv()
-                if d in rings(hop, k):
-                    go(ring(d, hop, k))
+    def onward(k):
+        for d in range(2):
+            ring(d, 1, k).wait_recv()
+            go(ring(d, 2, k))
+            if d in rings(3, k):
+                go(ring(d, 3, k))
+
+    onward(0)
+    edge_left.wait_recv()
+    edge_right.wait_recv()
+    send(2)
+    onward(1)
+    onward(2)
 
     me = y * NC + core
 
@@ -242,41 +258,28 @@
     origin = (me, low, high, far)
 
     def line(kind, k):
-        if kind == 0:
-            slot, peer = me, up_y
-        elif kind == 1:
-            slot, peer = me, dn_y
-        else:
-            slot, peer = (low, up_y) if UP[k] else (high, dn_y)
-        return remote(hold(slot, k), hold(slot, k), ysem.at[kind, k], peer)
+        return remote(hold(me, k), hold(me, k), ysem.at[kind, k], (up_y, dn_y, far_y)[kind])
 
     def across(n, k):
         return remote(hold(origin[n], k), hold(origin[n], k), csem.at[n, k], other)
 
     for k in range(3):
         at, size = CHUNKS[k]
-        for d in rings(3, k):
-            ring(d, 3, k).wait_recv()
         total = pack[at:at + size]
-        for hop in range(3):
-            total += zu[hop, at:at + size] + zd[hop, at:at + size]
+        for far in (0, 2, 3):
+            for d in rings(far, k):
+                ring(d, far, k).wait_recv()
+        for far in range(3):
+            total += zu[far, at:at + size] + zd[far, at:at + size]
         total += (zu if UP[k] else zd)[3, at:at + size]
         gath[me, at:at + size] = total
-        go(line(0, k))
-        go(line(1, k))
+        for kind in (2, 0, 1):
+            go(line(kind, k))
         go(across(0, k))
     for k in range(3):
-        line(0, k).wait_recv()
-        if UP[k]:
-            go(line(2, k))
-        go(across(1, k))
-        line(1, k).wait_recv()
-        if not UP[k]:
-            go(line(2, k))
-        go(across(2, k))
-    for k in range(3):
-        line(2, k).wait_recv()
-        go(across(3, k))
+        for kind in range(3):
+            line(kind, k).wait_recv()
+            go(across(1 + kind, k))
     for n in range(4):
         for k in range(3):
             across(n, k).wait_recv()
@@ -329,7 +332,7 @@
             dma((4, 3, 2)),
         ],
         compiler_params=pltpu.CompilerParams(
-            collective_id=0, has_side_effects=True, vmem_limit_bytes=40 << 20
+            collective_id=0, has_side_effects=True, vmem_limit_bytes=63 << 20
         ),
         name="gather",
     )(traces, fir, index)
@@ -389,7 +392,7 @@
             pltpu.VMEM((K, 256), BF),
         ],
         compiler_params=pltpu.CompilerParams(
-            dimension_semantics=("arbitrary",), vmem_limit_bytes=60 << 20
+            dimension_semantics=("arbitrary",), vmem_limit_bytes=63 << 20
         ),
         name="corr",
     )(src_ext, nr)

time: 68.6 us -> 58 us (0.85)
  Pallas kernels: 64.5 us -> 57.9 us
  local copies, waits for them, and re-layouts: 3.95 us -> 0 us
    pallas_call x1, Pallas kernels: 39.4 us -> 32.8 us  [gather(): pl.pallas_call(gather_kernel, in_specs=[pl.BlockSpec(memory_space=pl.ANY)...]
    unnamed x10 -> x0, local copies, waits for them, and re-layouts: 3.95 us -> none
where the time goes in v2:
time: 58 us; the launch traced here: 57.9 us
  Pallas kernels  57.9 us (100%)
    pallas_call x1, Pallas kernels, gather(): pl.pallas_call(gather_kernel, in_specs=[pl.BlockSpec(memory_space=pl.ANY)...  32.8 us
    pallas_call x1, Pallas kernels, corr(): pl.pallas_call(corr_kernel, grid=(CHN // 8,), in_specs=[pl.BlockSpec((S,...  25.1 us

profile of v2, /device:TPU:1, one launch (start us, length us, event | category | flops | bytes accessed | tf_op | source)
XLA Modules:
  0.0 57.9 jit_solution(7574485863359746771)
XLA Ops:
  0.0 32.8 %gather.1 = (bf16[64,2560]{1,0:T(8,128)(2,1)}, f32[16,80,128]{2,1,0:T(8,128)}) custom-call(f32[80,2048]{1,0:T(8,128)} %traces.1, f32[65]{0:T(128)} %fir.1, s32[64]{0:T(128)} %index.1), custom_call_target="tpu_custom_call" | custom-call | tf_op jit(solution)/shard_map/gather/pallas_call | solution.py:297
  32.8 25.1 %corr.1 = f32[64,10,4,8,128]{4,3,2,1,0:T(8,128)} custom-call(bf16[64,2560]{1,0:T(8,128)(2,1)} %get-tuple-element.7.src_ref, f32[16,80,128]{2,1,0:T(8,128)} %get-tuple-element.8.nr_ref), custom_call_target="tpu_custom_call" | custom-call | tf_op jit(solution)/shard_map/corr/pallas_call | solution.py:380

commit v3 on v2

--- a/solution.py
+++ b/solution.py
@@ -15,7 +15,10 @@
 SLOTS = 12
 NB = T // 128
 NP = T // 256
-K = T + 128
+KB = NB + 3
+K = KB * 128
+STEP = 16
+WIDE = 2
 AXES = ("chan_0", "chan_1", "chan_2", "tm")
 NZ, NY, NC, NX = 8, 4, 2, 4
 CHUNKS = ((0, 48), (48, 48), (96, 32))
@@ -226,10 +229,9 @@
     go(edge_right)
     fold(1)
     send(1)
-    turned = dot(nb[...], band[6])
+    turned = dot(nb[...], band[6]).astype(BF)
     for p in range(NP):
-        for h in range(2):
-            nrev[(NP - 1 - p) * 2 + h] = turned[p * CHN:(p + 1) * CHN, h * 128:h * 128 + 128]
+        nrev[:, (NP - 1 - p) * 256:(NP - p) * 256] = turned[p * CHN:(p + 1) * CHN]
     save = pltpu.make_async_copy(nrev, nr_out, lsem.at[1])
     save.start()
 
@@ -284,9 +286,10 @@
         for k in range(3):
             across(n, k).wait_recv()
 
-    spread = dot(unp[...], gath[...].reshape(8 * ROWS, 256)).astype(BF)
+    spread = dot(unp[...], gath[...].reshape(8 * ROWS, 256))
     for e in range(NP + 2):
-        src_out[:, e * 256:(e + 1) * 256] = spread[e * S:(e + 1) * S]
+        for h in range(2):
+            src_out[2 * e + h] = spread[e * S:(e + 1) * S, h * 128:h * 128 + 128]
     for copy in started:
         copy.wait_send()
     save.wait()
@@ -303,8 +306,8 @@
         ],
         out_specs=[pl.BlockSpec(memory_space=pltpu.VMEM), pl.BlockSpec(memory_space=pl.ANY)],
         out_shape=[
-            jax.ShapeDtypeStruct((S, T + 2 * LAG_HALF), BF),
-            jax.ShapeDtypeStruct((NB, CHN, 128), F32),
+            jax.ShapeDtypeStruct((NB + 4, S, 128), F32),
+            jax.ShapeDtypeStruct((CHN, T), BF),
         ],
         scratch_shapes=[
             pltpu.VMEM((CHN, T), F32),
@@ -316,7 +319,7 @@
             pltpu.VMEM(((NP + 1) * CHN, 256), BF),
             pltpu.VMEM(((NP + 1) * CHN, 256), BF),
             pltpu.VMEM((NP * CHN, 256), BF),
-            pltpu.VMEM((NB, CHN, 128), F32),
+            pltpu.VMEM((CHN, T), BF),
             pltpu.VMEM((4, 48, CHN), BF),
             pltpu.VMEM((2, 16, 256), BF),
             pltpu.VMEM((ROWS, 256), BF),
@@ -342,61 +345,70 @@
     g = pl.program_id(0)
     keep = iota((128, 128), 1) > iota((128, 128), 0)
 
-    def build(h, c, half):
+    def build(h, s, half):
         cols = slice(half * 128, half * 128 + 128)
-        prev = jnp.zeros((128, 128), F32)
-        for q in range(NB + 1):
-            b = NB - q
-            if b >= 1:
-                x = nr_ref.at[b - 1][pl.ds(c, 128, stride=0), :]
-                cur = pltpu.roll(x, 1, 1, stride=1, stride_axis=0)
-            else:
-                cur = jnp.zeros((128, 128), F32)
+
+        def turn(b):
+            x = src_ref.at[b][pl.ds(s, 128, stride=0), :]
+            return pltpu.roll(x, 1, 1, stride=1, stride_axis=0)
+
+        prev = turn(KB)
+        for q in range(KB):
+            cur = turn(KB - 1 - q)
             h[q * 128:(q + 1) * 128, cols] = jnp.where(keep, prev, cur).astype(BF)
             prev = cur
 
     @pl.when(g == 0)
     def _():
+        w_ref[...] = jnp.zeros_like(w_ref)
         for a in range(4):
-            w_ref[a * S:(a + 1) * S, :] = src_ref[:, a * 128:a * 128 + K]
-        build(h0, 0, 0)
-        build(h0, 1, 1)
-
-    out2 = o_ref.reshape(S * 4 * 8, 128)
+            w_ref[a * CHN:(a + 1) * CHN, (3 - a) * 128:(3 - a) * 128 + T] = nr_ref[...]
+        for i in range(WIDE):
+            build(h0, i, i)
+
     bufs = (h0, h1)
-    for p in range(4):
-        nxt = lax.rem(g * 8 + 2 * p + 2, CHN)
-        build(bufs[(p + 1) % 2], nxt, 0)
-        build(bufs[(p + 1) % 2], nxt + 1, 1)
-        res = dot(w_ref[...], bufs[p % 2][...]) * (1.0 / math.sqrt(T))
+    for p in range(STEP // WIDE):
+        nxt = lax.rem(g * STEP + WIDE * (p + 1), S)
+        for i in range(WIDE):
+            build(bufs[(p + 1) % 2], nxt + i, i)
+        h = bufs[p % 2]
+        res = dot(w_ref[:, 256:2048], h[256:2048, :])
+        low = dot(w_ref[2 * CHN:, 0:256], h[0:256, :])
+        high = dot(w_ref[:3 * CHN, 2048:2304], h[2048:2304, :])
+        last = dot(w_ref[:CHN, 2304:], h[2304:, :])
+        parts = [res[a * CHN:(a + 1) * CHN] for a in range(4)]
+        for a in (2, 3):
+            parts[a] += low[(a - 2) * CHN:(a - 1) * CHN]
+        for a in (0, 1, 2):
+            parts[a] += high[a * CHN:(a + 1) * CHN]
+        parts[0] += last
         for a in range(4):
-            for hh in range(2):
-                out2[pl.ds(a * 8 + 2 * p + hh, S, stride=32), :] = res[
-                    a * S:(a + 1) * S, hh * 128:hh * 128 + 128
-                ]
+            for i in range(WIDE):
+                o_ref[WIDE * p + i, :, a * 128:(a + 1) * 128] = parts[a][
+                    :, i * 128:(i + 1) * 128
+                ] * (1.0 / math.sqrt(T))
 
 
 def corr(src_ext, nr):
-    out = pl.pallas_call(
+    return pl.pallas_call(
         corr_kernel,
-        grid=(CHN // 8,),
+        grid=(S // STEP,),
         in_specs=[
-            pl.BlockSpec((S, T + 2 * LAG_HALF), lambda g: (0, 0)),
-            pl.BlockSpec((NB, CHN, 128), lambda g: (0, 0, 0)),
+            pl.BlockSpec((KB + 1, S, 128), lambda g: (0, 0, 0)),
+            pl.BlockSpec((CHN, T), lambda g: (0, 0)),
         ],
-        out_specs=pl.BlockSpec((S, 1, 4, 8, 128), lambda g: (0, g, 0, 0, 0)),
-        out_shape=jax.ShapeDtypeStruct((S, CHN // 8, 4, 8, 128), F32),
+        out_specs=pl.BlockSpec((STEP, CHN, 2 * LAG_HALF), lambda g: (g, 0, 0)),
+        out_shape=jax.ShapeDtypeStruct((S, CHN, 2 * LAG_HALF), F32),
         scratch_shapes=[
-            pltpu.VMEM((4 * S, K), BF),
-            pltpu.VMEM((K, 256), BF),
-            pltpu.VMEM((K, 256), BF),
+            pltpu.VMEM((4 * CHN, K), BF),
+            pltpu.VMEM((K, WIDE * 128), BF),
+            pltpu.VMEM((K, WIDE * 128), BF),
         ],
         compiler_params=pltpu.CompilerParams(
             dimension_semantics=("arbitrary",), vmem_limit_bytes=63 << 20
         ),
         name="corr",
     )(src_ext, nr)
-    return out.transpose(0, 1, 3, 2, 4).reshape(S, CHN, 2 * LAG_HALF)
 
 
 def body(traces, fir_taps, source_index):

time: 58 us -> 50.6 us (0.87)
  Pallas kernels: 57.9 us -> 50.5 us
    pallas_call x1, Pallas kernels: 25.1 us -> 17.6 us  [corr(): pl.pallas_call(corr_kernel, grid=(S // STEP,), in_specs=[pl.BlockSpec((KB...]
where the time goes in v3:
time: 50.6 us; the launch traced here: 50.5 us
  Pallas kernels  50.5 us (100%)
    pallas_call x1, Pallas kernels, gather(): pl.pallas_call(gather_kernel, in_specs=[pl.BlockSpec(memory_space=pl.ANY)...  32.9 us
    pallas_call x1, Pallas kernels, corr(): pl.pallas_call(corr_kernel, grid=(S // STEP,), in_specs=[pl.BlockSpec((KB...  17.6 us

profile of v3, /device:TPU:1, one launch (start us, length us, event | category | flops | bytes accessed | tf_op | source)
XLA Modules:
  0.0 50.5 jit_solution(17861115645773548923)
XLA Ops:
  0.0 32.9 %gather.1 = (f32[20,64,128]{2,1,0:T(8,128)}, bf16[80,2048]{1,0:T(8,128)(2,1)}) custom-call(f32[80,2048]{1,0:T(8,128)} %traces.1, f32[65]{0:T(128)} %fir.1, s32[64]{0:T(128)} %index.1), custom_call_target="tpu_custom_call" | custom-call | tf_op jit(solution)/shard_map/gather/pallas_call | solution.py:300
  32.9 17.6 %corr.1 = f32[64,80,512]{2,1,0:T(8,128)} custom-call(f32[20,64,128]{2,1,0:T(8,128)} %get-tuple-element.7.src_ref, bf16[80,2048]{1,0:T(8,128)(2,1)} %get-tuple-element.8.nr_ref), custom_call_target="tpu_custom_call" | custom-call | tf_op jit(solution)/shard_map/corr/pallas_call | solution.py:393

commit v4 on v3

--- a/solution.py
+++ b/solution.py
@@ -18,7 +18,8 @@
 KB = NB + 3
 K = KB * 128
 STEP = 16
-WIDE = 2
+WIDE = 4
+VA, VB = 16, 24
 AXES = ("chan_0", "chan_1", "chan_2", "tm")
 NZ, NY, NC, NX = 8, 4, 2, 4
 CHUNKS = ((0, 48), (48, 48), (96, 32))
@@ -42,8 +43,8 @@
 
 
 def gather_kernel(
-    traces, fir, index, src_out, nr_out,
-    xbuf, halo, xh, xl, band, fbuf, fa, fb, nb, nrev, pick, edge, pack, zu, zd, gath, unp,
+    traces, fir_in, index_in, src_out, nr_out,
+    fir, index, xbuf, halo, xh, xl, band, fbuf, fa, fb, nb, pick, edge, pack, zu, zd, gath, unp,
     lsem, hsem, esem, zsem, ysem, csem,
 ):
     z, y, core, x = (lax.axis_index(a) for a in AXES)
@@ -60,6 +61,10 @@
 
     load = pltpu.make_async_copy(traces, xbuf, lsem.at[0])
     load.start()
+    taps_load = pltpu.make_async_copy(fir_in, fir, lsem.at[1])
+    taps_load.start()
+    index_load = pltpu.make_async_copy(index_in, index, lsem.at[2])
+    index_load.start()
     barrier = pltpu.get_barrier_semaphore()
     peers = (up2_z, dn2_z, up_z, dn_z, far_y, up_y, dn_y, other, right, left)
     for peer in peers:
@@ -77,6 +82,8 @@
     to_right.start()
     to_left.start()
 
+    taps_load.wait()
+    index_load.wait()
     lane = iota((8, 128), 1)
     taps = jnp.zeros((8, 128), F32)
     for k in range(TAPS):
@@ -231,9 +238,7 @@
     send(1)
     turned = dot(nb[...], band[6]).astype(BF)
     for p in range(NP):
-        nrev[:, (NP - 1 - p) * 256:(NP - p) * 256] = turned[p * CHN:(p + 1) * CHN]
-    save = pltpu.make_async_copy(nrev, nr_out, lsem.at[1])
-    save.start()
+        nr_out[:, (NP - 1 - p) * 256:(NP - p) * 256] = turned[p * CHN:(p + 1) * CHN]
 
     def onward(k):
         for d in range(2):
@@ -292,7 +297,6 @@
             src_out[2 * e + h] = spread[e * S:(e + 1) * S, h * 128:h * 128 + 128]
     for copy in started:
         copy.wait_send()
-    save.wait()
 
 
 def gather(traces, fir, index):
@@ -300,16 +304,18 @@
     return pl.pallas_call(
         gather_kernel,
         in_specs=[
-            pl.BlockSpec(memory_space=pl.ANY),
-            pl.BlockSpec(memory_space=pltpu.SMEM),
-            pl.BlockSpec(memory_space=pltpu.SMEM),
+            pl.BlockSpec(memory_space=pltpu.HBM),
+            pl.BlockSpec(memory_space=pltpu.HBM),
+            pl.BlockSpec(memory_space=pltpu.HBM),
         ],
-        out_specs=[pl.BlockSpec(memory_space=pltpu.VMEM), pl.BlockSpec(memory_space=pl.ANY)],
+        out_specs=[pl.BlockSpec(memory_space=pltpu.VMEM)] * 2,
         out_shape=[
             jax.ShapeDtypeStruct((NB + 4, S, 128), F32),
             jax.ShapeDtypeStruct((CHN, T), BF),
         ],
         scratch_shapes=[
+            pltpu.SMEM((TAPS,), F32),
+            pltpu.SMEM((S,), jnp.int32),
             pltpu.VMEM((CHN, T), F32),
             pltpu.VMEM((2, CHN, 128), F32),
             pltpu.VMEM(((NP + 2) * CHN, 256), BF),
@@ -319,7 +325,6 @@
             pltpu.VMEM(((NP + 1) * CHN, 256), BF),
             pltpu.VMEM(((NP + 1) * CHN, 256), BF),
             pltpu.VMEM((NP * CHN, 256), BF),
-            pltpu.VMEM((CHN, T), BF),
             pltpu.VMEM((4, 48, CHN), BF),
             pltpu.VMEM((2, 16, 256), BF),
             pltpu.VMEM((ROWS, 256), BF),
@@ -327,7 +332,7 @@
             pltpu.VMEM((4, ROWS, 256), BF),
             pltpu.VMEM((8, ROWS, 256), BF),
             pltpu.VMEM(((NP + 2) * S, 8 * ROWS), BF),
-            dma((2,)),
+            dma((3,)),
             dma((2, 2)),
             dma((2, 2)),
             dma((2, 4, 3, 2)),
@@ -335,10 +340,10 @@
             dma((4, 3, 2)),
         ],
         compiler_params=pltpu.CompilerParams(
-            collective_id=0, has_side_effects=True, vmem_limit_bytes=63 << 20
+            collective_id=0, has_side_effects=True, vmem_limit_bytes=VA << 20
         ),
         name="gather",
-    )(traces, fir, index)
+    )(*(pltpu.with_memory_space_constraint(v, pltpu.HBM) for v in (traces, fir, index)))
 
 
 def corr_kernel(src_ref, nr_ref, o_ref, w_ref, h0, h1):
@@ -394,8 +399,8 @@
         corr_kernel,
         grid=(S // STEP,),
         in_specs=[
-            pl.BlockSpec((KB + 1, S, 128), lambda g: (0, 0, 0)),
-            pl.BlockSpec((CHN, T), lambda g: (0, 0)),
+            pl.BlockSpec(memory_space=pltpu.VMEM),
+            pl.BlockSpec(memory_space=pltpu.VMEM),
         ],
         out_specs=pl.BlockSpec((STEP, CHN, 2 * LAG_HALF), lambda g: (g, 0, 0)),
         out_shape=jax.ShapeDtypeStruct((S, CHN, 2 * LAG_HALF), F32),
@@ -405,7 +410,7 @@
             pltpu.VMEM((K, WIDE * 128), BF),
         ],
         compiler_params=pltpu.CompilerParams(
-            dimension_semantics=("arbitrary",), vmem_limit_bytes=63 << 20
+            dimension_semantics=("arbitrary",), vmem_limit_bytes=VB << 20
         ),
         name="corr",
     )(src_ext, nr)

time: 50.6 us -> 47.2 us (0.933)
  Pallas kernels: 50.5 us -> 47.1 us
    pallas_call x2, Pallas kernels: 50.5 us -> 47.1 us  [the longest x1 31.2 us: gather(): pl.pallas_call(gather_kernel, in_specs=[pl.BlockSpec(memory_space=pltpu.H...]
where the time goes in v4:
time: 47.2 us; the launch traced here: 47.1 us
  Pallas kernels  47.1 us (100%)
    pallas_call x1, Pallas kernels, gather(): pl.pallas_call(gather_kernel, in_specs=[pl.BlockSpec(memory_space=pltpu.H...  31.2 us
    pallas_call x1, Pallas kernels, corr(): pl.pallas_call(corr_kernel, grid=(S // STEP,), in_specs=[pl.BlockSpec(mem...  15.9 us

profile of v4, /device:TPU:1, one launch (start us, length us, event | category | flops | bytes accessed | tf_op | source)
XLA Modules:
  0.0 47.1 jit_solution(316518917083753660)
XLA Ops:
  0.0 31.2 %gather.1 = (f32[20,64,128]{2,1,0:T(8,128)S(1)}, bf16[80,2048]{1,0:T(8,128)(2,1)S(1)}) custom-call(f32[80,2048]{1,0:T(8,128)} %traces.1, f32[65]{0:T(128)} %fir_in.1, s32[64]{0:T(128)} %index_in.1), custom_call_target="tpu_custom_call" | custom-call | tf_op jit(solution)/shard_map/gather/pallas_call | solution.py:304
  31.2 15.9 %corr.1 = f32[64,80,512]{2,1,0:T(8,128)} custom-call(f32[20,64,128]{2,1,0:T(8,128)S(1)} %get-tuple-element.7.src_ref, bf16[80,2048]{1,0:T(8,128)(2,1)S(1)} %get-tuple-element.8.nr_ref), custom_call_target="tpu_custom_call" | custom-call | tf_op jit(solution)/shard_map/corr/pallas_call | solution.py:398

commit v5 on v4

--- a/solution.py
+++ b/solution.py
@@ -87,19 +87,19 @@
     lane = iota((8, 128), 1)
     taps = jnp.zeros((8, 128), F32)
     for k in range(TAPS):
-        taps = jnp.where(lane == k, fir[k], taps)
+        taps = jnp.where(lane == k, fir[TAPS - 1 - k], taps)
     rolled = pltpu.roll(jnp.concatenate([taps] * 16, axis=0), 128 - FIR_HALF, 1, stride=1, stride_axis=0)
     apart = iota((128, 128), 1) - iota((128, 128), 0)
     zero = jnp.zeros((128, 128), F32)
-    d1 = jnp.where(apart >= 128 - FIR_HALF, rolled, zero)
+    d1 = jnp.where(apart <= FIR_HALF - 128, rolled, zero)
     d2 = jnp.where(jnp.abs(apart) <= FIR_HALF, rolled, zero)
-    d3 = jnp.where(apart <= FIR_HALF - 128, rolled, zero)
-    for n, blocks in enumerate((((d1, d2), (zero, d1)), ((d3, zero), (d2, d3)))):
-        for i in range(2):
-            for u in range(2):
-                whole = blocks[i][u]
+    d3 = jnp.where(apart >= 128 - FIR_HALF, rolled, zero)
+    for n, blocks in enumerate((((d1, zero), (d2, d1)), ((d3, d2), (zero, d3)))):
+        for u in range(2):
+            for i in range(2):
+                whole = blocks[u][i]
                 high = whole.astype(BF)
-                at = (slice(i * 128, i * 128 + 128), slice(u * 128, u * 128 + 128))
+                at = (slice(u * 128, u * 128 + 128), slice(i * 128, i * 128 + 128))
                 band[(2 * n,) + at] = high
                 band[(2 * n + 1,) + at] = (whole - high.astype(F32)).astype(BF)
     gap = iota((256, 256), 0) - iota((256, 256), 1)
@@ -107,7 +107,19 @@
     none = jnp.zeros((256, 256), F32)
     band[4] = jnp.where((gap >= NORM_HALF) & (gap <= 3 * NORM_HALF), one, none).astype(BF)
     band[5] = jnp.where((gap <= -NORM_HALF) & (gap >= -3 * NORM_HALF), one, none).astype(BF)
-    band[6] = jnp.where(iota((256, 256), 0) + iota((256, 256), 1) == 255, one, none).astype(BF)
+
+    def put(group, half, block):
+        high = block.astype(BF)
+        at = (slice(group * CHN, group * CHN + CHN), slice(half * 128, half * 128 + 128))
+        xh[at] = high
+        xl[at] = (block - high.astype(F32)).astype(BF)
+
+    load.wait()
+    for b in range(NB):
+        put(1 + b // 2, b % 2, xbuf[:, b * 128:b * 128 + 128])
+    nothing = jnp.zeros((CHN, 128), F32)
+    put(0, 0, nothing)
+    put(NP + 1, 1, nothing)
 
     own = (z * NY + y) * NC + core
     lanes = iota((128, 128), 1)
@@ -127,6 +139,99 @@
         slot = jnp.where(inside & (subf == rank + SLOTS * i), fone, fnone).astype(BF)[0:48]
         pick[i] = dot_t(slot, hit).astype(BF)
 
+    def rows_of(ref, groups):
+        return jnp.concatenate([ref[lo * CHN:hi * CHN] for lo, hi in groups], axis=0)
+
+    def after(groups):
+        return [(lo + 1, hi + 1) for lo, hi in groups]
+
+    def filtered(groups):
+        high = [rows_of(xh, groups), rows_of(xh, after(groups))]
+        low = [rows_of(xl, groups), rows_of(xl, after(groups))]
+        taken = jnp.concatenate(high + low + high, axis=1)
+        return dot(taken, jnp.concatenate([band[n] for n in (0, 2, 0, 2, 1, 3)], axis=0))
+
+    def keep(lo, hi, value):
+        n = slice(lo * CHN, hi * CHN)
+        fbuf[n] = value
+        size = jnp.abs(value)
+        high = size.astype(BF)
+        fa[n] = high
+        fb[n] = (size - high.astype(F32)).astype(BF)
+
+    def normalize(groups):
+        taken = [rows_of(ref, part) for ref in (fa, fb) for part in (groups, after(groups))]
+        level = dot(
+            jnp.concatenate(taken, axis=1),
+            jnp.concatenate([band[n] for n in (4, 5, 4, 5)], axis=0),
+        )
+        below = EPSILON + level / (2 * NORM_HALF + 1)
+        at = 0
+        for lo, hi in groups:
+            size = (hi - lo) * CHN
+            first, second = slice(lo * CHN, hi * CHN), slice((lo + 1) * CHN, (hi + 1) * CHN)
+            nb[first, 0:128] = (fbuf[first, 128:256] / below[at:at + size, 0:128]).astype(BF)
+            nb[first, 128:256] = (fbuf[second, 0:128] / below[at:at + size, 128:256]).astype(BF)
+            at += size
+
+    def pair(p):
+        return nb[p * CHN:(p + 1) * CHN]
+
+    def fold(j):
+        total = dot(pick[0], pair(ORDER[4 * j]))
+        for i in range(1, 4):
+            total += dot(pick[i], pair(ORDER[4 * j + i]))
+        pack[48 * j:48 * j + 48, :] = total.astype(BF)
+
+    def part(ref, k):
+        at, size = CHUNKS[k]
+        return ref.at[at:at + size]
+
+    def ring(d, far, k):
+        slots, two, near = (zu, up2_z, up_z) if d == 0 else (zd, dn2_z, dn_z)
+        src = part(pack, k) if far < 2 else part(slots.at[1], k)
+        peer = (near, two, near, two)[far]
+        return remote(src, part(slots.at[far], k), zsem.at[d, far, k], peer)
+
+    def rings(far, k):
+        return [d for d in range(2) if far < 3 or (d == 0) == UP[k]]
+
+    started = [to_right, to_left]
+
+    def go(copy):
+        copy.start()
+        started.append(copy)
+
+    def send(k):
+        for far in (1, 0):
+            for d in range(2):
+                go(ring(d, far, k))
+
+    keep(1, NP, filtered([(1, NP)]))
+    normalize([(1, NP - 1)])
+    fold(0)
+    send(0)
+    to_right.wait_recv()
+    to_left.wait_recv()
+    put(0, 1, jnp.where(x > 0, halo[0], nothing))
+    put(NP + 1, 0, jnp.where(x < NX - 1, halo[1], nothing))
+    ends = iota((CHN, 256), 1)
+    empty = jnp.zeros((CHN, 256), F32)
+    both = filtered([(0, 1), (NP, NP + 1)])
+    keep(0, 1, jnp.where((ends >= 128) | (x > 0), both[0:CHN], empty))
+    keep(NP, NP + 1, jnp.where((ends < 128) | (x < NX - 1), both[CHN:], empty))
+    normalize([(0, 1), (NP - 1, NP)])
+    lower = dot(pick[0], pair(0))[0:16]
+    upper = dot(pick[0], pair(NP - 1))[0:16]
+    edge[0] = jnp.where(x > 0, lower, jnp.zeros_like(lower)).astype(BF)
+    edge[1] = jnp.where(x < NX - 1, upper, jnp.zeros_like(upper)).astype(BF)
+
+    edge_left = remote(edge.at[0], pack.at[112:128], esem.at[0], left)
+    edge_right = remote(edge.at[1], pack.at[96:112], esem.at[1], right)
+    go(edge_left)
+    go(edge_right)
+    fold(1)
+    send(1)
     colsum = jnp.sum(jnp.where(subs == lanes, rows.astype(F32), fnone), axis=1, keepdims=True)
     owner_col = jnp.floor((colsum + 0.5) * (1.0 / CHN))
     owner_row = jnp.floor((rows.astype(F32) + 0.5) * (1.0 / CHN))
@@ -141,101 +246,7 @@
         offset = 96 if e == 0 else 112 if e == NP + 1 else SLOTS * ORDER.index(e - 1)
         unp[e * S:(e + 1) * S, :] = jnp.where(wide == place + offset, uone, unone).astype(BF)
 
-    def put(group, half, block):
-        high = block.astype(BF)
-        at = (slice(group * CHN, group * CHN + CHN), slice(half * 128, half * 128 + 128))
-        xh[at] = high
-        xl[at] = (block - high.astype(F32)).astype(BF)
-
-    load.wait()
-    for b in range(NB):
-        put(1 + b // 2, b % 2, xbuf[:, b * 128:b * 128 + 128])
-    nothing = jnp.zeros((CHN, 128), F32)
-    put(0, 0, nothing)
-    put(NP + 1, 1, nothing)
-
-    def filtered(lo, hi):
-        n = slice(lo * CHN, hi * CHN)
-        m = slice((lo + 1) * CHN, (hi + 1) * CHN)
-        value = dot_t(xh[n], band[0]) + dot_t(xh[m], band[2])
-        value += dot_t(xl[n], band[0]) + dot_t(xl[m], band[2])
-        value += dot_t(xh[n], band[1]) + dot_t(xh[m], band[3])
-        return value
-
-    def keep(lo, hi, value):
-        n = slice(lo * CHN, hi * CHN)
-        fbuf[n] = value
-        size = jnp.abs(value)
-        high = size.astype(BF)
-        fa[n] = high
-        fb[n] = (size - high.astype(F32)).astype(BF)
-
-    def normalize(lo, hi):
-        first, second = slice(lo * CHN, hi * CHN), slice((lo + 1) * CHN, (hi + 1) * CHN)
-        level = dot(fa[first], band[4]) + dot(fa[second], band[5])
-        level += dot(fb[first], band[4]) + dot(fb[second], band[5])
-        below = EPSILON + level / (2 * NORM_HALF + 1)
-        nb[first, 0:128] = (fbuf[first, 128:256] / below[:, 0:128]).astype(BF)
-        nb[first, 128:256] = (fbuf[second, 0:128] / below[:, 128:256]).astype(BF)
-
-    def pair(p):
-        return nb[p * CHN:(p + 1) * CHN]
-
-    def fold(j):
-        total = dot(pick[0], pair(ORDER[4 * j]))
-        for i in range(1, 4):
-            total += dot(pick[i], pair(ORDER[4 * j + i]))
-        pack[48 * j:48 * j + 48, :] = total.astype(BF)
-
-    def part(ref, k):
-        at, size = CHUNKS[k]
-        return ref.at[at:at + size]
-
-    def ring(d, far, k):
-        slots, two, near = (zu, up2_z, up_z) if d == 0 else (zd, dn2_z, dn_z)
-        src = part(pack, k) if far < 2 else part(slots.at[1], k)
-        peer = (near, two, near, two)[far]
-        return remote(src, part(slots.at[far], k), zsem.at[d, far, k], peer)
-
-    def rings(far, k):
-        return [d for d in range(2) if far < 3 or (d == 0) == UP[k]]
-
-    started = [to_right, to_left]
-
-    def go(copy):
-        copy.start()
-        started.append(copy)
-
-    def send(k):
-        for far in (1, 0):
-            for d in range(2):
-                go(ring(d, far, k))
-
-    keep(1, NP, filtered(1, NP))
-    normalize(1, NP - 1)
-    fold(0)
-    send(0)
-    to_right.wait_recv()
-    to_left.wait_recv()
-    put(0, 1, jnp.where(x > 0, halo[0], nothing))
-    put(NP + 1, 0, jnp.where(x < NX - 1, halo[1], nothing))
-    ends = iota((CHN, 256), 1)
-    empty = jnp.zeros((CHN, 256), F32)
-    keep(0, 1, jnp.where((ends >= 128) | (x > 0), filtered(0, 1), empty))
-    keep(NP, NP + 1, jnp.where((ends < 128) | (x < NX - 1), filtered(NP, NP + 1), empty))
-    normalize(0, 1)
-    normalize(NP - 1, NP)
-    lower = dot(pick[0], pair(0))[0:16]
-    upper = dot(pick[0], pair(NP - 1))[0:16]
-    edge[0] = jnp.where(x > 0, lower, jnp.zeros_like(lower)).astype(BF)
-    edge[1] = jnp.where(x < NX - 1, upper, jnp.zeros_like(upper)).astype(BF)
-
-    edge_left = remote(edge.at[0], pack.at[112:128], esem.at[0], left)
-    edge_right = remote(edge.at[1], pack.at[96:112], esem.at[1], right)
-    go(edge_left)
-    go(edge_right)
-    fold(1)
-    send(1)
+    band[6] = jnp.where(iota((256, 256), 0) + iota((256, 256), 1) == 255, one, none).astype(BF)
     turned = dot(nb[...], band[6]).astype(BF)
     for p in range(NP):
         nr_out[:, (NP - 1 - p) * 256:(NP - p) * 256] = turned[p * CHN:(p + 1) * CHN]

time: 47.2 us -> 47 us (level)
  no operation moved by 1% of the time
where the time goes in v5:
time: 47 us
  Pallas kernels  47 us (100%)
    pallas_call x1, Pallas kernels, gather(): pl.pallas_call(gather_kernel, in_specs=[pl.BlockSpec(memory_space=pltpu.H...  31.1 us
    pallas_call x1, Pallas kernels, corr(): pl.pallas_call(corr_kernel, grid=(S // STEP,), in_specs=[pl.BlockSpec(mem...  15.9 us

profile of v5, /device:TPU:1, one launch (start us, length us, event | category | flops | bytes accessed | tf_op | source)
XLA Modules:
  0.0 47.0 jit_solution(17674033624750344369)
XLA Ops:
  0.0 31.1 %gather.1 = (f32[20,64,128]{2,1,0:T(8,128)S(1)}, bf16[80,2048]{1,0:T(8,128)(2,1)S(1)}) custom-call(f32[80,2048]{1,0:T(8,128)} %traces.1, f32[65]{0:T(128)} %fir_in.1, s32[64]{0:T(128)} %index_in.1), custom_call_target="tpu_custom_call" | custom-call | tf_op jit(solution)/shard_map/gather/pallas_call | solution.py:315
  31.1 15.9 %corr.1 = f32[64,80,512]{2,1,0:T(8,128)} custom-call(f32[20,64,128]{2,1,0:T(8,128)S(1)} %get-tuple-element.7.src_ref, bf16[80,2048]{1,0:T(8,128)(2,1)S(1)} %get-tuple-element.8.nr_ref), custom_call_target="tpu_custom_call" | custom-call | tf_op jit(solution)/shard_map/corr/pallas_call | solution.py:409

commit v6 on v5

--- a/solution.py
+++ b/solution.py
@@ -239,7 +239,9 @@
         jnp.where((owner_row == owner_col) & (lanes < subs), fone, fnone), axis=1, keepdims=True
     )
     residue = owner_col - 8.0 * jnp.floor(owner_col * 0.125)
-    place = (residue * ROWS + rank_col)[0:S]
+    line_of = jnp.floor(residue * 0.5)
+    other_core = jnp.abs(residue - 2.0 * line_of - core.astype(F32))
+    place = ((line_of + NY * other_core) * ROWS + rank_col)[0:S]
     wide = iota((S, 8 * ROWS), 1).astype(F32)
     uone, unone = jnp.ones((S, 8 * ROWS), F32), jnp.zeros((S, 8 * ROWS), F32)
     for e in range(NP + 2):
@@ -265,21 +267,20 @@
     onward(1)
     onward(2)
 
-    me = y * NC + core
+    me = y
 
     def hold(slot, k):
         at, size = CHUNKS[k]
         return gath.at[slot, at:at + size]
 
-    low, high = lax.rem(y + NY - 1, NY) * NC + core, lax.rem(y + 1, NY) * NC + core
-    far = lax.rem(y + 2, NY) * NC + core
+    low, high, far = lax.rem(y + NY - 1, NY), lax.rem(y + 1, NY), lax.rem(y + 2, NY)
     origin = (me, low, high, far)
 
     def line(kind, k):
         return remote(hold(me, k), hold(me, k), ysem.at[kind, k], (up_y, dn_y, far_y)[kind])
 
     def across(n, k):
-        return remote(hold(origin[n], k), hold(origin[n], k), csem.at[n, k], other)
+        return remote(hold(origin[n], k), hold(NY + origin[n], k), csem.at[n, k], other)
 
     for k in range(3):
         at, size = CHUNKS[k]
@@ -298,14 +299,23 @@
         for kind in range(3):
             line(kind, k).wait_recv()
             go(across(1 + kind, k))
+    half = NY * ROWS
+
+    def spread(half_of, slots):
+        at = half_of * half
+        return dot(unp[:, at:at + half], gath[slots].reshape(half, 256))
+
+    near = spread(0, slice(0, NY))
+    for e in range(NP + 2):
+        for h in range(2):
+            src_out[2 * e + h] = near[e * S:(e + 1) * S, h * 128:h * 128 + 128]
     for n in range(4):
         for k in range(3):
             across(n, k).wait_recv()
-
-    spread = dot(unp[...], gath[...].reshape(8 * ROWS, 256))
+    rest = spread(1, slice(NY, 2 * NY))
     for e in range(NP + 2):
         for h in range(2):
-            src_out[2 * e + h] = spread[e * S:(e + 1) * S, h * 128:h * 128 + 128]
+            src_out[2 * e + h] += rest[e * S:(e + 1) * S, h * 128:h * 128 + 128]
     for copy in started:
         copy.wait_send()
 

time: 47 us -> 46.9 us (level)
  no operation moved by 1% of the time
where the time goes in v6:
time: 46.9 us; the launch traced here: 46.8 us
  Pallas kernels  46.8 us (100%)
    pallas_call x1, Pallas kernels, gather(): pl.pallas_call(gather_kernel, in_specs=[pl.BlockSpec(memory_space=pltpu.H...  30.9 us
    pallas_call x1, Pallas kernels, corr(): pl.pallas_call(corr_kernel, grid=(S // STEP,), in_specs=[pl.BlockSpec(mem...  15.9 us

profile of v6, /device:TPU:1, one launch (start us, length us, event | category | flops | bytes accessed | tf_op | source)
XLA Modules:
  0.0 46.8 jit_solution(9224788003242725463)
XLA Ops:
  0.0 30.9 %gather.1 = (f32[20,64,128]{2,1,0:T(8,128)S(1)}, bf16[80,2048]{1,0:T(8,128)(2,1)S(1)}) custom-call(f32[80,2048]{1,0:T(8,128)} %traces.1, f32[65]{0:T(128)} %fir_in.1, s32[64]{0:T(128)} %index_in.1), custom_call_target="tpu_custom_call" | custom-call | tf_op jit(solution)/shard_map/gather/pallas_call | solution.py:325
  30.9 15.9 %corr.1 = f32[64,80,512]{2,1,0:T(8,128)} custom-call(f32[20,64,128]{2,1,0:T(8,128)S(1)} %get-tuple-element.7.src_ref, bf16[80,2048]{1,0:T(8,128)(2,1)S(1)} %get-tuple-element.8.nr_ref), custom_call_target="tpu_custom_call" | custom-call | tf_op jit(solution)/shard_map/corr/pallas_call | solution.py:419
